TPU v7x, 512 devices: a whole 4x4x16 slice. The times are simulated.
512 devices in a mesh: prow: 16 (over y_hi, x, core), pcol: 32 (over y_lo, z).
Axes of the slice: x: 4, y: 4 (y_hi: 2, y_lo: 2; y = y_hi * 2 + y_lo), z: 16, core: 2. Of those that a mesh axis runs over, the one named last changes fastest.
Arguments:
- sep_inverse: bfloat16 [2, 16, 256, 1, 32, 256], P(None, 'prow', None, None, 'pcol'), may hold values from -2 to 30, as said below
- panels: bfloat16 [4, 2, 16, 256, 256], P(None, None, 'prow', 'pcol'), may hold values from -0.0625 to 0.0625
- ancestors: int32 [4, 32], replicated, may hold values from 0 to 1, as said below
- window_factor: bfloat16 [6, 256, 256], replicated, may hold values from -0.1875 to 0.1875
- diag_inverse: bfloat16 [4, 256, 256], replicated, may hold values from -1 to 4, as said below
Outputs:
- ys: float32 [4, 2, 16, 256, 256], P(None, None, 'prow', 'pcol')
- window_inverse: float32 [1024, 1024], P('prow', 'pcol')
Inputs may be any that keep to these rules, and one draw needn't show every extreme that they name: sep_inverse read as in the first step is symmetric. `diag_inverse`: each block is symmetric. ancestors[k + 1, t] <= ancestors[k, t]: a supernode's ancestor tiles lie among those of the one before it.
All inputs are finite; a program needn't handle non-finite values.
Results may differ from a plain program's by a relative error of at most 0.00035.
Values may be sent and summed in bfloat16 or wider, within the bound.
A program may use at most 64 MiB of HBM per device.

v0:
```python
import jax
import jax.numpy as jnp
from jax import lax
from jax.sharding import PartitionSpec as P


def broadcast(block, axis, owner):
    block = jnp.where(lax.axis_index(axis) == owner, block, jnp.zeros_like(block))
    return lax.psum(block, axis)


def product(operand_left, operand_right):
    return jnp.dot(
        operand_left,
        operand_right,
        precision=lax.Precision.HIGHEST,
        preferred_element_type=jnp.float32,
    )


def pair_index(earlier, later):
    return later * (later - 1) // 2 + earlier


def window_step(later, window_sums, window_factor, diag_inverse, window_blocks):
    coupled = []
    for earlier in range(later):
        running = window_sums[earlier]
        for partner in range(later):
            running = running + product(
                window_blocks[earlier, partner],
                window_factor[pair_index(partner, later)].astype(jnp.float32),
            )
        upper_block = -running
        window_blocks[earlier, later] = upper_block
        window_blocks[later, earlier] = upper_block.T
        coupled.append(upper_block)
    running = window_sums[later]
    for earlier in range(later):
        running = running + product(
            window_factor[pair_index(earlier, later)].astype(jnp.float32).T, coupled[earlier]
        )
    window_blocks[later, later] = diag_inverse[later].astype(jnp.float32) - running


def assemble_window(window_blocks, supernodes):
    return jnp.block(
        [
            [window_blocks[first, second] for second in range(supernodes)]
            for first in range(supernodes)
        ]
    )


def per_device(sep_inverse, panels, ancestors, window_factor, diag_inverse):
    prow_count = lax.axis_size("prow")
    pcol_count = lax.axis_size("pcol")
    row_index = lax.axis_index("prow")
    column_index = lax.axis_index("pcol")
    tile_rows = sep_inverse.shape[0]
    width = sep_inverse.shape[2]
    owned_count = sep_inverse.shape[3]
    supernodes = panels.shape[0]
    slice_rows = panels.shape[3]
    group_ratio = pcol_count // prow_count
    local_sep = sep_inverse.reshape(tile_rows, width, owned_count, width)
    window_blocks = {}
    columns = []
    for later in range(supernodes):
        tile_flags = lax.dynamic_slice_in_dim(
            ancestors[later].reshape(tile_rows, prow_count), row_index, 1, 1
        )
        keep_tiles = tile_flags.astype(jnp.bfloat16).reshape(tile_rows, 1, 1)
        own_piece = panels[later, :, 0] * keep_tiles
        full_rows = lax.all_gather(own_piece, "pcol", axis=1, tiled=True)
        grouped = full_rows.reshape(owned_count, group_ratio, width, width)
        picked = lax.dynamic_slice_in_dim(grouped, column_index // prow_count, 1, 1)[:, 0]
        owned_tiles = broadcast(picked, "prow", column_index % prow_count)

        def row_term(first_row, row_count, owned_tiles=owned_tiles):
            return jnp.einsum(
                "rbcd,cde->bre", local_sep, owned_tiles, preferred_element_type=jnp.float32
            )

        summed = lax.psum_scatter(
            row_term(jnp.int32(0), slice_rows * lax.axis_size("pcol")),
            "pcol",
            scatter_dimension=0,
            tiled=True,
        )
        row_total = jnp.transpose(summed, (1, 0, 2)).reshape(tile_rows * slice_rows, width)
        row_keep = jnp.repeat(
            tile_flags[:, 0].astype(jnp.float32),
            slice_rows,
            total_repeat_length=tile_rows * slice_rows,
        )
        carried = -row_total
        for earlier in range(later):
            carried = carried - product(
                columns[earlier], window_factor[pair_index(earlier, later)].astype(jnp.float32)
            )
        current = carried * row_keep[:, None]
        factor_rows = own_piece.reshape(tile_rows * slice_rows, width).astype(jnp.float32)
        window_parts = [product(columns[earlier].T, factor_rows) for earlier in range(later)]
        window_parts.append(product(factor_rows.T, current))
        window_sums = lax.psum(jnp.stack(window_parts), ("prow", "pcol"))
        window_step(later, window_sums, window_factor, diag_inverse, window_blocks)
        columns.append(current)
    ys = jnp.stack(columns).reshape(supernodes, tile_rows, 1, slice_rows, width)
    whole_window = assemble_window(window_blocks, supernodes)
    rows_each = supernodes * width // prow_count
    cols_each = supernodes * width // pcol_count
    local_window = lax.dynamic_slice(
        whole_window, (row_index * rows_each, column_index * cols_each), (rows_each, cols_each)
    )
    return (ys, local_window)


def solution(mesh):
    placed = (
        P(None, "prow", None, None, "pcol", None),
        P(None, None, "prow", "pcol", None),
        P(),
        P(),
        P(),
    )
    return jax.shard_map(
        per_device,
        mesh=mesh,
        in_specs=placed,
        out_specs=(P(None, None, "prow", "pcol", None), P("prow", "pcol")),
        check_vma=False,
    )
```

profile of v0, /device:TPU:4, one launch (start us, length us, event | category | flops | bytes accessed | tf_op | source)
XLA Modules:
  0.0 1206.1 jit_solution(4849116906709062268)
XLA Ops:
  7.3 0.8 slice_reduce_fusion.1
  8.9 0.8 bitcast_multiply_fusion.6
  9.8 70.2 %all_gather.12 = bf16[2,256,256]{2,0,1:T(2,128)(2,1)S(1)} all-gather(bf16[2,8,256]{2,0,1:T(2,128)(2,1)S(1)} %copy.58), channel_id=1, replica_groups=mesh['prow'=16,'pcol'=32] {'pcol'}, dimensions={1}, use_global_device_ids=true | all-gather | bytes 270336 | tf_op jit(solution)/shard_map/all_gather | solution.py:75
  80.4 59.8 %all_gather.13 = bf16[2,256,256]{2,0,1:T(2,128)(2,1)S(1)} all-gather(bf16[2,8,256]{2,0,1:T(2,128)(2,1)S(1)} %copy.63), channel_id=1, replica_groups=mesh['prow'=16,'pcol'=32] {'pcol'}, dimensions={1}, use_global_device_ids=true | all-gather | bytes 270336 | tf_op jit(solution)/shard_map/all_gather | solution.py:75
  140.7 0.7 select_bitcast_fusion.3
  141.3 0.6 select_bitcast_fusion.2
  142.0 61.7 %all_gather.15 = bf16[2,256,256]{2,0,1:T(2,128)(2,1)S(1)} all-gather(bf16[2,8,256]{2,0,1:T(2,128)(2,1)S(1)} %copy.73), channel_id=1, replica_groups=mesh['prow'=16,'pcol'=32] {'pcol'}, dimensions={1}, use_global_device_ids=true | all-gather | bytes 270336 | tf_op jit(solution)/shard_map/all_gather | solution.py:75
  204.1 0.7 select_bitcast_fusion
  204.8 59.8 %all_gather.14 = bf16[2,256,256]{2,0,1:T(2,128)(2,1)S(1)} all-gather(bf16[2,8,256]{2,0,1:T(2,128)(2,1)S(1)} %copy.68), channel_id=1, replica_groups=mesh['prow'=16,'pcol'=32] {'pcol'}, dimensions={1}, use_global_device_ids=true | all-gather | bytes 270336 | tf_op jit(solution)/shard_map/all_gather | solution.py:75
  265.0 0.7 select_bitcast_fusion.1
  265.8 141.1 %all-reduce.15.cloned.1.call-done = (bf16[256,256]{0,1:T(8,128)(2,1)}, bf16[256,256]{0,1:T(8,128)(2,1)}, bf16[256,256]{0,1:T(8,128)(2,1)}, bf16[256,256]{0,1:T(8,128)(2,1)}) async-done(((bf16[256,256]{0,1:T(8,128)(2,1)}, bf16[256,256]{0,1:T(8,128)(2,1)}, bf16[256,256]{0,1:T(8,128)(2,1)}, bf16[256,256]{0,1:T(8,128)(2,1)}), (bf16[256,256]{0,1:T(8,128)(2,1)}, bf16[256,256]{0,1:T(8,128)(2,1)}, ...) | async-done | bytes 524304 | tf_op jit(solution)/shard_map/psum | solution.py:9
  406.9 1.2 convolution_bitcast_fusion
  408.1 1.0 copy.75
  409.3 1.0 copy.60
  410.6 1.0 copy.65
  411.9 1.0 copy.70
  414.1 0.6 fusion.134
  414.7 0.6 fusion.135
  415.3 0.7 fusion.136
  415.9 0.6 fusion.137
  416.5 5.0 broadcast_select_fusion
  421.6 1.3 dynamic-slice.31
  423.5 262.1 %all-reduce.13.cloned.1.call-done = (f32[256,2,256]{2,1,0:T(2,128)}, f32[256,2,256]{2,1,0:T(2,128)}, f32[256,2,256]{2,1,0:T(2,128)}, f32[256,2,256]{2,1,0:T(2,128)}) async-done(((f32[256,2,256]{2,1,0:T(2,128)}, f32[256,2,256]{2,1,0:T(2,128)}, f32[256,2,256]{2,1,0:T(2,128)}, f32[256,2,256]{2,1,0:T(2,128)}), (f32[256,2,256]{2,1,0:T(2,128)}, f32[256,2,256]{2,1,0:T(2,128)}, f32[256,2,256]{2,1,0:T(2,128)}, ...) | async-done | bytes 2097168
  685.7 0.7 constant_dynamic-slice_fusion.11
  686.4 0.4 convolution_bitcast_fusion.13
  686.8 0.4 convolution_bitcast_fusion.16
  687.2 0.4 convolution_bitcast_fusion.18
  687.6 1.1 convolution_bitcast_fusion.19
  688.7 0.7 constant_dynamic-slice_fusion.10
  689.4 0.7 constant_dynamic-slice_fusion.9
  690.5 0.3 convolution_bitcast_fusion.15
  691.0 0.4 convolution_bitcast_fusion.14
  691.5 0.3 convolution_bitcast_fusion.11
  691.8 0.3 convolution_bitcast_fusion.12
  692.1 0.7 constant_dynamic-slice_fusion.8
  693.2 0.4 convolution_bitcast_fusion.17
  693.8 0.4 convolution_bitcast_fusion.10
  694.2 0.8 pad_maximum_fusion.2
  695.0 0.9 pad_maximum_fusion.1
  696.0 1.1 pad_maximum_fusion
  697.2 0.6 pad_maximum_fusion.3
  697.8 481.1 %all-reduce.11.cloned.1.call-done = (f32[1,256,256]{2,1,0:T(8,128)}, f32[4,256,256]{2,1,0:T(8,128)}, f32[2,256,256]{2,1,0:T(8,128)}, f32[3,256,256]{2,1,0:T(8,128)}) async-done(((f32[1,256,256]{2,1,0:T(8,128)}, f32[4,256,256]{2,1,0:T(8,128)}, f32[2,256,256]{2,1,0:T(8,128)}, f32[3,256,256]{2,1,0:T(8,128)}), (f32[1,256,256]{2,1,0:T(8,128)}, f32[4,256,256]{2,1,0:T(8,128)}, f32[2,256,256]{2,1,0:T(8,128)}, ...) | async-done | bytes 2621456 | tf_op jit(solution)/shard_map/psum | solution.py:106
  1178.9 1.0 subtract_bitcast_fusion
  1179.9 1.3 fusion.14
  1181.2 0.3 fusion.11
  1181.6 0.4 convolution_add_fusion.5
  1182.2 0.4 copy-done.5
  1182.7 0.4 convolution_add_fusion.7
  1183.6 1.0 fusion.7
  1184.7 0.4 convolution_add_fusion.2
  1185.1 0.8 copy.82
  1186.7 0.9 copy.86
  1187.6 0.9 copy.91
  1189.0 0.4 copy-done.4
  1189.4 1.2 fusion.6
  1190.6 0.8 copy.85
  1191.4 2.0 fusion.3
  1193.4 0.8 copy.90
  1194.3 0.4 convolution_add_fusion.1
  1194.7 0.6 copy-done.3
  1195.2 0.3 fusion.2
  1195.8 1.9 fusion.1
  1197.9 1.1 maximum_maximum_fusion
  1198.9 0.7 copy.93
  (76 shorter events, 8.4 us)
Async XLA Ops:
  7.2 399.7 %copy-start = (bf16[2,1,256,1,1,256]{5,2,4,3,1,0:T(8,128)(2,1)S(1)}, bf16[2,1,256,1,1,256]{5,2,4,3,1,0:T(8,128)(2,1)}, u32[]{:S(2)}) copy-start(bf16[2,1,256,1,1,256]{5,2,4,3,1,0:T(8,128)(2,1)} %param.15) | copy-start | bytes 786436
  7.2 399.7 %all-reduce.15.cloned.1.call-start = ((), (), s32[]{:S(2)}) async-start(), calls=%async_computation.2 | async-start | bytes 1048576 | tf_op jit(solution)/shard_map/psum | solution.py:9
  265.7 420.0 %all-reduce.13.cloned.1.call-start = ((), (), s32[]{:S(2)}) async-start(), calls=%async_computation.1 | async-start | bytes 4194304
  406.9 2.2 copy-start.11
  409.1 1.3 copy-start.10
  410.3 1.3 copy-start.9
  412.9 3.6 copy-start.12
  412.9 273.5 %copy-start.8 = (bf16[4,2,1,8,256]{4,3,2,1,0:T(8,128)(2,1)S(1)}, bf16[4,2,1,8,256]{4,3,2,1,0:T(8,128)(2,1)}, u32[]{:S(2)}) copy-start(bf16[4,2,1,8,256]{4,3,2,1,0:T(8,128)(2,1)} %param.16) | copy-start | bytes 98308
  412.9 277.2 %copy-start.1 = (bf16[6,256,256]{2,1,0:T(8,128)(2,1)S(1)}, bf16[6,256,256]{2,1,0:T(8,128)(2,1)}, u32[]{:S(2)}) copy-start(bf16[6,256,256]{2,1,0:T(8,128)(2,1)} %param.18) | copy-start | bytes 2359300
  412.9 765.9 %all-reduce.11.cloned.1.call-start = ((), (), s32[]{:S(2)}) async-start(), calls=%async_computation | async-start | bytes 5242880 | tf_op jit(solution)/shard_map/psum | solution.py:106
  697.1 481.8 %copy-start.7 = (bf16[4,256,256]{2,1,0:T(8,128)(2,1)S(1)}, bf16[4,256,256]{2,1,0:T(8,128)(2,1)}, u32[]{:S(2)}) copy-start(bf16[4,256,256]{2,1,0:T(8,128)(2,1)} %param.19) | copy-start | bytes 1572868
  1178.9 2.4 copy-start.6
  1179.9 1.7 copy-start.2
  1181.6 1.1 copy-start.5
  1188.4 0.9 copy-start.4
  1194.3 0.9 copy-start.3
Sparse Core Ops, SparseCore 0:
  265.8 140.9 all-reduce.14
  413.1 272.5 all-reduce.12
  697.2 481.5 all-reduce.10
where the time goes:
time: 1210 us
  waiting for transfers between devices  884 us (73%)
  blocking collectives  252 us (21%)
  local copies, waits for them, and re-layouts  20.5 us (2%)
  matrix products  19.6 us (2%)
  other arithmetic  15 us (1%)
  between operations  14.9 us (1%)
    psum x1, waiting for transfers between devices, per_device(): window_sums = lax.psum(jnp.stack(window_parts), ('prow', 'pcol'))  481 us
    unnamed x4, waiting for transfers between devices  262 us
    all_gather x4, blocking collectives, per_device(): full_rows = lax.all_gather(own_piece, 'pcol', axis=1, tiled=True)  252 us
    psum x1, waiting for transfers between devices, broadcast(): return lax.psum(block, axis)  141 us
  transfers between devices with their start and end apart: 3, of which 3 were waited for; matrix products, arithmetic and copies ran while one was open for 1% of the time, Pallas kernels for 0%

commit v1 on v0

--- a/solution.py
+++ b/solution.py
@@ -2,6 +2,11 @@
 import jax.numpy as jnp
 from jax import lax
 from jax.sharding import PartitionSpec as P
+
+
+def all_by_exchange(value, mesh_axis, along):
+    sent = jnp.stack([value] * lax.axis_size(mesh_axis))
+    return jnp.concatenate(lax.all_to_all(sent, mesh_axis, 0, 0), axis=along)
 
 
 def broadcast(block, axis, owner):
@@ -72,7 +77,7 @@
         )
         keep_tiles = tile_flags.astype(jnp.bfloat16).reshape(tile_rows, 1, 1)
         own_piece = panels[later, :, 0] * keep_tiles
-        full_rows = lax.all_gather(own_piece, "pcol", axis=1, tiled=True)
+        full_rows = all_by_exchange(own_piece, "pcol", 1)
         grouped = full_rows.reshape(owned_count, group_ratio, width, width)
         picked = lax.dynamic_slice_in_dim(grouped, column_index // prow_count, 1, 1)[:, 0]
         owned_tiles = broadcast(picked, "prow", column_index % prow_count)

time: 1210 us -> 1060 us (0.88)
  blocking collectives: 252 us -> 63.5 us
  waiting for transfers between devices: 884 us -> 922 us
    all_gather x4 -> x0, blocking collectives: 252 us -> none  [per_device(): full_rows = lax.all_gather(own_piece, 'pcol', axis=1, tiled=True)]
    all_to_all x0 -> x2, blocking collectives: none -> 63.5 us  [all_by_exchange(): return jnp.concatenate(lax.all_to_all(sent, mesh_axis, 0, 0), axis=along)]
    all_to_all x0 -> x2, waiting for transfers between devices: none -> 38.5 us  [all_by_exchange(): return jnp.concatenate(lax.all_to_all(sent, mesh_axis, 0, 0), axis=along)]
  transfers between devices with their start and end apart: 3 -> 5, of which waited for: 3 -> 5; matrix products, arithmetic and copies ran while one was open for 1% -> 1% of each run, Pallas kernels for 0% -> 0%
where the time goes in v1:
time: 1060 us
  waiting for transfers between devices  922 us (87%)
  blocking collectives  63.5 us (6%)
  local copies, waits for them, and re-layouts  20.8 us (2%)
  matrix products  19.6 us (2%)
  other arithmetic  15 us (1%)
  between operations  14.9 us (1%)
    psum x1, waiting for transfers between devices, per_device(): window_sums = lax.psum(jnp.stack(window_parts), ('prow', 'pcol'))  481 us
    unnamed x4, waiting for transfers between devices  262 us
    psum x1, waiting for transfers between devices, broadcast(): return lax.psum(block, axis)  141 us
    all_to_all x2, blocking collectives, all_by_exchange(): return jnp.concatenate(lax.all_to_all(sent, mesh_axis, 0, 0), axis=along)  63.5 us
    all_to_all x2, waiting for transfers between devices, all_by_exchange(): return jnp.concatenate(lax.all_to_all(sent, mesh_axis, 0, 0), axis=along)  38.5 us
  transfers between devices with their start and end apart: 5, of which 5 were waited for; matrix products, arithmetic and copies ran while one was open for 1% of the time, Pallas kernels for 0%

profile of v1, /device:TPU:4, one launch (start us, length us, event | category | flops | bytes accessed | tf_op | source)
XLA Modules:
  0.0 1063.5 jit_solution(8696860600660960613)
XLA Ops:
  7.2 0.8 slice_reduce_fusion.1
  8.8 0.8 bitcast_multiply_fusion.6
  9.7 38.5 %all_to_all.20 = bf16[32,2,8,256]{3,2,1,0:T(8,128)(2,1)S(1)} all-to-all(bf16[32,2,8,256]{3,2,1,0:T(8,128)(2,1)S(1)} %stack.45), channel_id=1, replica_groups=mesh['prow'=16,'pcol'=32] {'pcol'}, dimensions={0} | all-to-all | bytes 524288 | tf_op jit(solution)/shard_map/all_to_all | solution.py:9
  48.2 24.9 %all_to_all.21 = bf16[32,2,8,256]{3,2,1,0:T(8,128)(2,1)S(1)} all-to-all(bf16[32,2,8,256]{3,2,1,0:T(8,128)(2,1)S(1)} %stack.43), channel_id=1, replica_groups=mesh['prow'=16,'pcol'=32] {'pcol'}, dimensions={0} | all-to-all | bytes 524288 | tf_op jit(solution)/shard_map/all_to_all | solution.py:9
  73.2 0.7 stack.42
  73.9 3.9 all-to-all-start
  77.8 20.9 %all-to-all-done = bf16[32,2,8,256]{3,2,1,0:T(8,128)(2,1)S(1)} async-done(((bf16[32,2,8,256]{3,2,1,0:T(8,128)(2,1)}), bf16[32,2,8,256]{3,2,1,0:T(8,128)(2,1)S(1)}, u32[]{:S(2)}, u32[]{:S(2)}) %all-to-all-start) | async-done | bytes 262176 | tf_op jit(solution)/shard_map/all_to_all | solution.py:9
  98.7 0.7 stack.47
  99.4 3.9 all-to-all-start.3
  103.8 0.7 select_bitcast_fusion.1
  104.5 0.7 select_bitcast_fusion.2
  105.1 0.7 select_bitcast_fusion.3
  105.8 17.6 %all-to-all-done.3 = bf16[32,2,8,256]{3,2,1,0:T(8,128)(2,1)S(1)} async-done(((bf16[32,2,8,256]{3,2,1,0:T(8,128)(2,1)}), bf16[32,2,8,256]{3,2,1,0:T(8,128)(2,1)S(1)}, u32[]{:S(2)}, u32[]{:S(2)}) %all-to-all-start.3) | async-done | bytes 262176 | tf_op jit(solution)/shard_map/all_to_all | solution.py:9
  123.5 0.7 select_bitcast_fusion
  124.3 140.5 %all-reduce.15.cloned.1.call-done = (bf16[256,256]{0,1:T(8,128)(2,1)}, bf16[256,256]{0,1:T(8,128)(2,1)}, bf16[256,256]{0,1:T(8,128)(2,1)}, bf16[256,256]{0,1:T(8,128)(2,1)}) async-done(((bf16[256,256]{0,1:T(8,128)(2,1)}, bf16[256,256]{0,1:T(8,128)(2,1)}, bf16[256,256]{0,1:T(8,128)(2,1)}, bf16[256,256]{0,1:T(8,128)(2,1)}), (bf16[256,256]{0,1:T(8,128)(2,1)}, bf16[256,256]{0,1:T(8,128)(2,1)}, ...) | async-done | bytes 524304 | tf_op jit(solution)/shard_map/psum | solution.py:14
  264.8 1.2 convolution_bitcast_fusion
  266.0 1.0 copy.64
  267.3 1.0 copy.52
  268.5 1.0 copy.56
  269.8 1.0 copy.60
  272.0 0.6 fusion.134
  272.6 0.6 fusion.135
  273.2 0.7 fusion.136
  273.9 0.6 fusion.137
  274.5 5.0 broadcast_select_fusion
  279.5 1.3 dynamic-slice.15
  281.5 261.8 %all-reduce.13.cloned.1.call-done = (f32[256,2,256]{2,1,0:T(2,128)}, f32[256,2,256]{2,1,0:T(2,128)}, f32[256,2,256]{2,1,0:T(2,128)}, f32[256,2,256]{2,1,0:T(2,128)}) async-done(((f32[256,2,256]{2,1,0:T(2,128)}, f32[256,2,256]{2,1,0:T(2,128)}, f32[256,2,256]{2,1,0:T(2,128)}, f32[256,2,256]{2,1,0:T(2,128)}), (f32[256,2,256]{2,1,0:T(2,128)}, f32[256,2,256]{2,1,0:T(2,128)}, f32[256,2,256]{2,1,0:T(2,128)}, ...) | async-done | bytes 2097168
  543.3 0.7 constant_dynamic-slice_fusion.11
  544.0 0.4 convolution_bitcast_fusion.13
  544.4 0.4 convolution_bitcast_fusion.16
  544.8 0.4 convolution_bitcast_fusion.18
  545.2 1.1 convolution_bitcast_fusion.19
  546.3 0.7 constant_dynamic-slice_fusion.10
  547.0 0.7 constant_dynamic-slice_fusion.9
  548.1 0.3 convolution_bitcast_fusion.15
  548.6 0.4 convolution_bitcast_fusion.14
  549.7 0.7 constant_dynamic-slice_fusion.8
  550.8 0.4 convolution_bitcast_fusion.17
  551.4 0.4 convolution_bitcast_fusion.10
  551.8 0.8 pad_maximum_fusion.2
  552.7 0.9 pad_maximum_fusion.1
  553.6 1.1 pad_maximum_fusion
  554.8 0.6 pad_maximum_fusion.3
  555.4 480.8 %all-reduce.11.cloned.1.call-done = (f32[1,256,256]{2,1,0:T(8,128)}, f32[4,256,256]{2,1,0:T(8,128)}, f32[2,256,256]{2,1,0:T(8,128)}, f32[3,256,256]{2,1,0:T(8,128)}) async-done(((f32[1,256,256]{2,1,0:T(8,128)}, f32[4,256,256]{2,1,0:T(8,128)}, f32[2,256,256]{2,1,0:T(8,128)}, f32[3,256,256]{2,1,0:T(8,128)}), (f32[1,256,256]{2,1,0:T(8,128)}, f32[4,256,256]{2,1,0:T(8,128)}, f32[2,256,256]{2,1,0:T(8,128)}, ...) | async-done | bytes 2621456 | tf_op jit(solution)/shard_map/psum | solution.py:111
  1036.2 1.0 subtract_bitcast_fusion
  1037.3 1.3 fusion.14
  1038.9 0.4 convolution_add_fusion.5
  1039.6 0.4 copy-done.5
  1040.1 0.4 convolution_add_fusion.7
  1041.0 1.0 fusion.7
  1042.0 0.4 convolution_add_fusion.2
  1042.4 0.8 copy.71
  1044.1 0.9 copy.75
  1044.9 0.9 copy.80
  1046.3 0.4 copy-done.4
  1046.7 1.2 fusion.6
  1048.0 0.8 copy.74
  1048.8 2.0 fusion.3
  1050.8 0.8 copy.79
  1051.6 0.4 convolution_add_fusion.1
  1052.0 0.6 copy-done.3
  1053.2 1.9 fusion.1
  1055.2 1.1 maximum_maximum_fusion
  1056.3 0.7 copy.82
  (82 shorter events, 8.5 us)
Async XLA Ops:
  7.2 257.6 %copy-start = (bf16[2,1,256,1,1,256]{5,2,4,3,1,0:T(8,128)(2,1)S(1)}, bf16[2,1,256,1,1,256]{5,2,4,3,1,0:T(8,128)(2,1)}, u32[]{:S(2)}) copy-start(bf16[2,1,256,1,1,256]{5,2,4,3,1,0:T(8,128)(2,1)} %param.15) | copy-start | bytes 786436
  73.9 24.9 %all-to-all-start = ((bf16[32,2,8,256]{3,2,1,0:T(8,128)(2,1)}), bf16[32,2,8,256]{3,2,1,0:T(8,128)(2,1)S(1)}, u32[]{:S(2)}, u32[]{:S(2)}) async-start(bf16[32,2,8,256]{3,2,1,0:T(8,128)(2,1)} %stack.42), calls=%async_computation | async-start | bytes 524288 | tf_op jit(solution)/shard_map/all_to_all | solution.py:9
  99.4 24.0 %all-to-all-start.3 = ((bf16[32,2,8,256]{3,2,1,0:T(8,128)(2,1)}), bf16[32,2,8,256]{3,2,1,0:T(8,128)(2,1)S(1)}, u32[]{:S(2)}, u32[]{:S(2)}) async-start(bf16[32,2,8,256]{3,2,1,0:T(8,128)(2,1)} %stack.47), calls=%async_computation.3 | async-start | bytes 524288 | tf_op jit(solution)/shard_map/all_to_all | solution.py:9
  103.3 161.5 %all-reduce.15.cloned.1.call-start = ((), (), s32[]{:S(2)}) async-start(), calls=%async_computation.6 | async-start | bytes 1048576 | tf_op jit(solution)/shard_map/psum | solution.py:14
  124.2 419.0 %all-reduce.13.cloned.1.call-start = ((), (), s32[]{:S(2)}) async-start(), calls=%async_computation.5 | async-start | bytes 4194304
  264.8 2.2 copy-start.11
  267.0 1.3 copy-start.10
  268.3 1.3 copy-start.9
  270.8 3.6 copy-start.12
  270.8 273.2 %copy-start.8 = (bf16[4,2,1,8,256]{4,3,2,1,0:T(8,128)(2,1)S(1)}, bf16[4,2,1,8,256]{4,3,2,1,0:T(8,128)(2,1)}, u32[]{:S(2)}) copy-start(bf16[4,2,1,8,256]{4,3,2,1,0:T(8,128)(2,1)} %param.16) | copy-start | bytes 98308
  270.9 276.8 %copy-start.1 = (bf16[6,256,256]{2,1,0:T(8,128)(2,1)S(1)}, bf16[6,256,256]{2,1,0:T(8,128)(2,1)}, u32[]{:S(2)}) copy-start(bf16[6,256,256]{2,1,0:T(8,128)(2,1)} %param.18) | copy-start | bytes 2359300
  270.9 765.3 %all-reduce.11.cloned.1.call-start = ((), (), s32[]{:S(2)}) async-start(), calls=%async_computation.4 | async-start | bytes 5242880 | tf_op jit(solution)/shard_map/psum | solution.py:111
  554.7 481.5 %copy-start.7 = (bf16[4,256,256]{2,1,0:T(8,128)(2,1)S(1)}, bf16[4,256,256]{2,1,0:T(8,128)(2,1)}, u32[]{:S(2)}) copy-start(bf16[4,256,256]{2,1,0:T(8,128)(2,1)} %param.19) | copy-start | bytes 1572868
  1036.2 2.4 copy-start.6
  1037.3 1.7 copy-start.2
  1038.9 1.1 copy-start.5
  1045.8 0.9 copy-start.4
  1051.6 0.9 copy-start.3
Sparse Core Ops, SparseCore 0:
  124.4 140.3 all-reduce.14
  271.0 272.2 all-reduce.12
  554.8 481.3 all-reduce.10
